TPU v7x, 512 devices: a whole 4x8x8 slice. The times are simulated.
512 devices in a mesh: samp: 32 (over x, z), blk: 16 (over y, core).
Axes of the slice: x: 4, y: 8, z: 8, core: 2. Of those that a mesh axis runs over, the one named last changes fastest.
Arguments:
- dosages: int32 [49152, 8192], P('samp', 'blk'), may hold values from 0 to 2, as said below
- new_dosages: int32 [49152, 2048], P('samp', 'blk'), may hold values from 0 to 2, as said below
- traits: float32 [64, 49152], P(None, 'samp'), may hold values from -40 to 40
- shrink: float32 [5], replicated, may hold values from 0.5 to 5
Outputs:
- residual: float32 [5, 64, 49152], P(None, 'blk', 'samp')
- scores: float32 [5, 64, 2048], P(None, None, 'blk')
Inputs may be any that keep to these rules, and one draw needn't show every extreme that they name: `dosages`: codes of haplotype pairs, with linkage along neighbouring variants. `new_dosages`: codes of haplotype pairs, with linkage along neighbouring variants.
All inputs are finite; a program needn't handle non-finite values.
Results may differ from a plain program's by a relative error of at most 0.0053.
Values may be sent and summed in bfloat16 or wider, within the bound.
No kernel may reach another device: no remote copies, remote signals or barrier semaphores. Data moves between devices by JAX's collectives and lax.ppermute only.
A program may use at most 64 MiB of HBM per device.

v0:
```python
import jax
import jax.numpy as jnp
from jax import lax
from jax.sharding import Mesh, PartitionSpec as P

RIDGE = 5
SAMP = ("x", "z")
BLK = ("y", "core")
FACTORS = {32: (4, 8), 16: (8, 2), 4: (2, 2)}
EPS = 1e-05
F32 = jnp.float32
BF16 = jnp.bfloat16


def dot(a, b, contract, precision=None):
    return lax.dot_general(
        a, b, (contract, ((), ())), precision=precision, preferred_element_type=F32
    )


def rounded(values):
    return lax.reduce_precision(values, 8, 7)


def column_stats(shifted_sum, shifted_sq, count):
    mean = (shifted_sum + count) / count
    var = (shifted_sq + 2.0 * shifted_sum + count) / count - mean * mean
    return (mean, 1.0 / jnp.sqrt(var + EPS))


def scaled(codes, mean, inv):
    return ((codes.astype(F32) - mean) * inv).astype(BF16)


def affine(shifted_sum, shifted_sq, mean, inv, count):
    low, mid, high = (rounded((code - mean) * inv) for code in (0.0, 1.0, 2.0))
    n_low = (shifted_sq - shifted_sum) * 0.5
    n_high = (shifted_sq + shifted_sum) * 0.5
    n_mid = count - shifted_sq
    value_mean = (n_low * low + n_mid * mid + n_high * high) / count
    pairs = n_low * n_mid + n_mid * n_high + 4.0 * n_low * n_high
    slopes = (
        n_low * n_mid * (mid - low)
        + n_mid * n_high * (high - mid)
        + 2.0 * n_low * n_high * (high - low)
    )
    slope = jnp.where(pairs > 0.0, slopes / jnp.maximum(pairs, 1.0), inv)
    square = (n_low * low * low + n_mid * mid * mid + n_high * high * high) / count
    return (value_mean, slope, square)


def chebyshev_coefficients(lam, bound):
    centre = lam + bound / 2.0
    half = bound / 2.0
    sig = centre / half
    q0 = 1.0 / sig
    d0 = 1.0 / centre
    r1a, r1b = (1.0 - lam * d0, -d0)
    q1 = 1.0 / (2.0 * sig - q0)
    step = 2.0 * q1 / half
    d1a, d1b = (q1 * q0 * d0 + step * r1a, step * r1b)
    r2a = r1a - lam * d1a
    r2b = r1b - d1a - lam * d1b
    r2c = -d1b
    q2 = 1.0 / (2.0 * sig - q1)
    step = 2.0 * q2 / half
    d2a, d2b, d2c = (q2 * q1 * d1a + step * r2a, q2 * q1 * d1b + step * r2b, step * r2c)
    return (d0 + d1a + d2a, d1b + d2b, d2c)


def shards(dosages, new_dosages, traits, shrink):
    rows, width = dosages.shape
    fresh_width = new_dosages.shape[1]
    trait_count = traits.shape[0]
    samp, blk = (lax.axis_size(SAMP), lax.axis_size(BLK))
    depth, cores, zs = (lax.axis_size("y"), lax.axis_size("core"), lax.axis_size("z"))
    count = float(rows * samp)
    half_width = width // 2
    share_rows = half_width // samp
    share = trait_count // blk
    columns = RIDGE * trait_count
    codes = (dosages - 1).astype(BF16)
    codes_f = (dosages - 1).astype(F32)
    new_f = (new_dosages - 1).astype(F32)
    trait_bf = traits.astype(BF16)
    parts = (
        jnp.sum(codes_f, axis=0),
        jnp.sum(codes_f * codes_f, axis=0),
        jnp.sum(new_f, axis=0),
        jnp.sum(new_f * new_f, axis=0),
        jnp.sum(trait_bf.astype(F32), axis=1),
    )
    sizes = [p.shape[0] for p in parts]
    slots = share_rows * 256
    sums = jnp.pad(jnp.concatenate(parts), (0, slots - sum(sizes))).reshape(share_rows, 256)
    first, second = (codes[:, :half_width], codes[:, half_width:])
    over_rows = ((0,), (0,))
    gram_top = dot(first, codes, over_rows)
    gram_low = dot(second, second, over_rows)
    cross = dot(codes, trait_bf, ((0,), (1,)))
    wide = 3 * half_width
    payload = jnp.concatenate(
        [gram_top, gram_low, cross[:half_width], cross[half_width:]], axis=1
    ).reshape(samp, share_rows, wide + 2 * trait_count)
    payload = jnp.concatenate(
        [payload, jnp.broadcast_to(sums[None], (samp, share_rows, 256))], axis=2
    )
    chunk = jnp.sum(lax.all_to_all(payload, SAMP, 0, 0, tiled=True), axis=0)
    totals = chunk[:, wide + 2 * trait_count :].reshape(slots)
    pieces, at = ([], 0)
    for size in sizes:
        pieces.append(totals[at : at + size])
        at += size
    code_sum, code_sq, new_sum, new_sq, trait_sum = pieces
    mean, inv = column_stats(code_sum, code_sq, count)
    value_mean, slope, square = affine(code_sum, code_sq, mean, inv, count)
    start = lax.axis_index(SAMP) * share_rows

    def own(vector, offset):
        return lax.dynamic_slice(vector, (start + offset,), (share_rows,))[:, None]

    def centred(product, offset, column_from):
        sums_i, slope_i, value_i = (own(v, offset) for v in (code_sum, slope, value_mean))
        out = (
            slope_i
            * slope[None, column_from:]
            * (product / count - sums_i / count * (code_sum[None, column_from:] / count))
        )
        out = out + value_i * value_mean[None, column_from:]
        row = start + offset + lax.broadcasted_iota(jnp.int32, out.shape, 0)
        column = column_from + lax.broadcasted_iota(jnp.int32, out.shape, 1)
        return jnp.where(row == column, 0.0, out)

    def centred_cross(product, offset):
        sums_i, slope_i, value_i = (own(v, offset) for v in (code_sum, slope, value_mean))
        trait_mean = trait_sum[None, :] / count
        return slope_i * (product / count - sums_i / count * trait_mean) + value_i * trait_mean

    rhs_rows = jnp.concatenate(
        [
            centred_cross(chunk[:, wide : wide + trait_count], 0),
            centred_cross(chunk[:, wide + trait_count : wide + 2 * trait_count], half_width),
        ],
        axis=1,
    )
    rhs_high = rounded(rhs_rows)
    own_rows = jnp.concatenate(
        [
            centred(chunk[:, :width], 0, 0),
            centred(chunk[:, width:wide], half_width, half_width),
            rhs_high,
            rhs_rows - rhs_high,
        ],
        axis=1,
    ).astype(BF16)
    every = lax.all_to_all(
        jnp.broadcast_to(own_rows[None], (samp, *own_rows.shape)), SAMP, 0, 0, tiled=True
    ).reshape(half_width, own_rows.shape[1])
    top_left, top_right = (every[:, :half_width], every[:, half_width:width])
    low_right = every[:, width:wide]
    gram = jnp.concatenate(
        [
            jnp.concatenate([top_left, top_right], axis=1),
            jnp.concatenate([top_right.T, low_right], axis=1),
        ],
        axis=0,
    )
    bound = jnp.max(jnp.sum(jnp.abs(gram.astype(F32)), axis=0) + square)
    rhs_parts = every[:, wide:].reshape(half_width, 2, 2, trait_count)
    rhs_parts = rhs_parts.transpose(1, 3, 2, 0).reshape(2 * trait_count, width)

    def apply_gram(high, low, whole):
        out = dot(jnp.concatenate([high, low], axis=0), gram, ((1,), (0,)))
        return out[:trait_count] + out[trait_count:] + square[None, :] * whole

    high, low = (rhs_parts[:trait_count], rhs_parts[trait_count:])
    rhs = high.astype(F32) + low.astype(F32)
    once = apply_gram(high, low, rhs)
    once_high = rounded(once)
    twice = apply_gram(once_high.astype(BF16), (once - once_high).astype(BF16), once)
    coefficients = chebyshev_coefficients(shrink, bound)
    row = lax.broadcasted_iota(jnp.int32, (columns, 3 * trait_count), 0)
    column = lax.broadcasted_iota(jnp.int32, (columns, 3 * trait_count), 1)
    side, in_side = (row // (columns // cores), row % (columns // cores))
    place, in_place = (in_side // (RIDGE * share), in_side % (RIDGE * share))
    ridge, in_share = (in_place // share, in_place % share)
    core = lax.rem(lax.axis_index("core") + 1 + side, cores)
    trait = (place * cores + core) * share + in_share
    mixing = jnp.zeros((columns, 3 * trait_count), F32)
    for power in range(3):
        for r in range(RIDGE):
            mixing = jnp.where(
                (ridge == r) & (column == trait + power * trait_count),
                coefficients[power][r],
                mixing,
            )
    weights = dot(
        mixing, jnp.concatenate([rhs, once, twice], axis=0), ((1,), (0,)), lax.Precision.HIGHEST
    ).astype(BF16)
    standard = scaled(dosages, mean, inv)
    new_mean, new_inv = column_stats(new_sum, new_sq, count)
    fresh = scaled(new_dosages, new_mean, new_inv)
    half_columns = columns // cores
    along = ((1,), (1,))
    sent = dot(weights[:half_columns], standard, along).astype(BF16)
    kept = dot(weights[half_columns:], standard, along)
    arrived = lax.ppermute(sent, "core", [(0, 1), (1, 0)])
    paired = (kept + arrived.astype(F32)).astype(BF16).reshape(depth, RIDGE * share, rows)
    summed = lax.all_to_all(paired, "y", 0, 0, tiled=True)
    pred = jnp.sum(summed.astype(F32), axis=0).reshape(RIDGE, share, rows)
    own_traits = lax.dynamic_slice_in_dim(traits, lax.axis_index(BLK) * share, share, 0)
    residual = own_traits[None] - pred
    res_bf = lax.all_gather(
        residual.astype(BF16).reshape(RIDGE * share, rows), BLK, axis=0, tiled=True
    )
    raw_part = dot(res_bf, fresh, ((1,), (0,)))
    res_float = res_bf.astype(F32)
    squares = jnp.sum(res_float * res_float, axis=1).reshape(zs, 1, columns // zs)
    squares = jnp.pad(squares, ((0, 0), (0, 7), (0, fresh_width - columns // zs)))
    ends = jnp.concatenate([raw_part.reshape(zs, columns // zs, fresh_width), squares], axis=1)
    ends = jnp.sum(lax.all_to_all(ends, "z", 0, 0, tiled=True), axis=0)
    ends = lax.psum(ends, "x")
    raw, sum_sq = (ends[: columns // zs], ends[columns // zs, : columns // zs])
    scores = raw / jnp.sqrt(count * (sum_sq / count + EPS))[:, None]
    scores = lax.all_to_all(
        jnp.broadcast_to(scores[None], (zs, *scores.shape)), "z", 0, 0, tiled=True
    )
    scores = scores.reshape(blk, RIDGE, share, fresh_width).transpose(1, 0, 2, 3)
    return (residual, scores.reshape(RIDGE, trait_count, fresh_width))


def solution(mesh):
    samp, blk = (FACTORS[mesh.shape["samp"]], FACTORS[mesh.shape["blk"]])
    grid = Mesh(mesh.devices.reshape(*samp, *blk), SAMP + BLK)
    return jax.shard_map(
        shards,
        mesh=grid,
        in_specs=(P(SAMP, BLK), P(SAMP, BLK), P(None, SAMP), P()),
        out_specs=(P(None, BLK, SAMP), P(None, None, BLK)),
        check_vma=False,
    )
```

profile of v0, /device:TPU:8, one launch (start us, length us, event | category | flops | bytes accessed | tf_op | source)
XLA Modules:
  0.0 220.9 jit_solution(13262179598304185275)
XLA Ops:
  0.6 2.3 %add_convert_fusion = bf16[1536,512]{1,0:T(8,128)(2,1)S(1)} fusion(s32[1536,512]{1,0:T(8,128)} %param.4), kind=kLoop, calls=%fused_computation.3 | loop fusion | flops 1572864 | bytes 4718592 | tf_op jit(solution)/shard_map/convert_element_type | solution.py:82
  3.0 1.4 fusion.2
  4.4 1.1 fusion
  5.6 0.6 multiply_reduce_fusion
  6.6 2.1 fusion.119
  8.8 0.7 fusion.171
  9.8 1.3 constant_dynamic-update-slice_fusion.4
  11.1 1.3 constant_dynamic-update-slice_fusion.3
  12.4 1.3 constant_dynamic-update-slice_fusion.2
  13.6 1.3 constant_dynamic-update-slice_fusion.1
  14.9 1.3 constant_dynamic-update-slice_fusion
  16.2 0.7 pad.8
  16.9 1.4 maximum_bitcast_fusion
  18.3 1.1 pad_maximum_fusion
  19.4 13.3 %all-to-all-start = ((f32[32,8,1152]{2,1,0:T(8,128)}), f32[32,8,1152]{2,1,0:T(8,128)}, u32[]{:S(2)}, u32[]{:S(2)}) async-start(f32[32,8,1152]{2,1,0:T(8,128)} %pad_maximum_fusion), calls=%async_computation | async-start | bytes 2359296 | tf_op jit(solution)/shard_map/all_to_all | solution.py:108
  32.7 0.5 iota_add_fusion.2
  33.2 0.5 iota_add_fusion.1
  33.7 30.3 %all-to-all-done = f32[32,8,1152]{2,1,0:T(8,128)} async-done(((f32[32,8,1152]{2,1,0:T(8,128)}), f32[32,8,1152]{2,1,0:T(8,128)}, u32[]{:S(2)}, u32[]{:S(2)}) %all-to-all-start) | async-done | bytes 1179680 | tf_op jit(solution)/shard_map/all_to_all | solution.py:108
  64.0 2.0 reduce_sum.97
  66.0 0.8 slice_bitcast_fusion.1
  67.0 0.7 slice_multiply_fusion.4
  67.7 0.8 fusion.131
  68.5 0.6 copy-done.8
  69.1 0.8 fusion.138
  69.9 0.8 fusion.126
  70.8 0.9 broadcast_in_dim.108
  71.6 5.3 %all-to-all-start.1 = ((bf16[32,8,1024]{2,1,0:T(8,128)(2,1)}), bf16[32,8,1024]{2,1,0:T(8,128)(2,1)}, u32[]{:S(2)}, u32[]{:S(2)}) async-start(bf16[32,8,1024]{2,1,0:T(8,128)(2,1)} %broadcast_in_dim.108), calls=%async_computation.1 | async-start | bytes 1048576 | tf_op jit(solution)/shard_map/all_to_all | solution.py:156
  77.0 0.6 fusion.148
  77.6 0.6 iota_divide_fusion
  78.2 0.6 fusion.145
  78.7 14.7 %all-to-all-done.1 = bf16[32,8,1024]{2,1,0:T(8,128)(2,1)} async-done(((bf16[32,8,1024]{2,1,0:T(8,128)(2,1)}), bf16[32,8,1024]{2,1,0:T(8,128)(2,1)}, u32[]{:S(2)}, u32[]{:S(2)}) %all-to-all-start.1) | async-done | bytes 524320 | tf_op jit(solution)/shard_map/all_to_all | solution.py:156
  93.5 1.8 fusion.170
  95.3 1.7 concatenate.57
  96.9 1.7 copy.34
  98.6 1.2 abs_reduce_fusion
  99.8 0.6 reduce_sum.99
  100.4 1.4 fusion.150
  102.4 0.7 negate_multiply_fusion
  103.0 0.7 add_add_fusion.1
  103.7 0.7 fusion.176
  104.4 0.7 fusion.177
  105.1 0.7 fusion.175
  105.7 1.7 copy.28
  107.4 0.9 fusion.172
  108.5 1.3 fusion.111
  110.6 11.3 %convolution_convert_fusion.1 = bf16[320,512]{1,0:T(8,128)(2,1)S(1)} fusion(f32[64,512]{1,0:T(8,128)S(1)} %fusion.109, f32[64,512]{1,0:T(8,128)S(1)} %get-tuple-element.14, f32[64,512]{1,0:T(8,128)S(1)} %get-tuple-element.20, f32[]{:T(128)} %bitcast.18, f32[]{:T(128)} %bitcast.17, f32[]{:T(128)} %bitcast.16, f32[]{:T(128)} %bitcast.15, f32[]{:T(128)} %bitcast.14, ...), kind=kOutput, calls=%fused_computation.6 | convolution fusion | flops 383008768 | bytes 726720 | tf_op jit(solution)/shard_map/dot_general | solution.py:16
  121.8 0.7 convolution_convert_fusion
  122.5 1.9 collective-permute-start
  124.5 1.8 collective-permute-done
  126.3 1.5 add_convert_fusion.1
  127.8 2.0 reshape.255
  129.8 7.5 %all-to-all-start.2 = ((bf16[8,20,1536]{2,1,0:T(8,128)(2,1)}), bf16[8,20,1536]{2,1,0:T(8,128)(2,1)S(1)}, u32[]{:S(2)}, u32[]{:S(2)}) async-start(bf16[8,20,1536]{2,1,0:T(8,128)(2,1)} %reshape.255), calls=%async_computation.2 | async-start | bytes 1179648 | tf_op jit(solution)/shard_map/all_to_all | solution.py:209
  137.4 0.8 add_multiply_fusion.4
  138.1 16.9 %all-to-all-done.2 = bf16[8,20,1536]{2,1,0:T(8,128)(2,1)S(1)} async-done(((bf16[8,20,1536]{2,1,0:T(8,128)(2,1)}), bf16[8,20,1536]{2,1,0:T(8,128)(2,1)S(1)}, u32[]{:S(2)}, u32[]{:S(2)}) %all-to-all-start.2) | async-done | bytes 491552 | tf_op jit(solution)/shard_map/all_to_all | solution.py:209
  155.2 19.1 %all-gather = bf16[16,20,1536]{2,1,0:T(8,128)(2,1)S(1)} all-gather(bf16[1,20,1536]{2,1,0:T(8,128)(2,1)S(1)} %fusion.121), channel_id=1, replica_groups=mesh['x'=4,'z'=8,'y'=8,'core'=2] {'y','core'}, dimensions={0}, use_global_device_ids=true | all-gather | bytes 1044480 | tf_op jit(solution)/shard_map/all_gather | solution.py:213
  175.3 0.7 select_maximum_fusion
  176.0 4.2 %all-to-all-start.3 = ((f32[8,48,128]{2,1,0:T(8,128)}), f32[8,48,128]{2,1,0:T(8,128)S(1)}, u32[]{:S(2)}, u32[]{:S(2)}) async-start(f32[8,48,128]{2,1,0:T(8,128)} %select_maximum_fusion), calls=%async_computation.3 | async-start | bytes 393216 | tf_op jit(solution)/shard_map/all_to_all | solution.py:221
  180.3 11.0 %all-to-all-done.3 = f32[8,48,128]{2,1,0:T(8,128)S(1)} async-done(((f32[8,48,128]{2,1,0:T(8,128)}), f32[8,48,128]{2,1,0:T(8,128)S(1)}, u32[]{:S(2)}, u32[]{:S(2)}) %all-to-all-start.3) | async-done | bytes 196640 | tf_op jit(solution)/shard_map/all_to_all | solution.py:221
  191.3 15.4 %psum.7 = f32[48,128]{1,0:T(8,128)S(1)} all-reduce(f32[48,128]{1,0:T(8,128)S(1)} %reduce_sum.102), channel_id=1, replica_groups=mesh['x'=4,'z'=8,'y'=8,'core'=2] {'x'}, use_global_device_ids=true, to_apply=%region_11.12 | all-reduce | flops 6144 | bytes 49152 | tf_op jit(solution)/shard_map/psum | solution.py:222
  206.8 0.7 broadcast_in_dim.125
  207.4 3.4 %all-to-all-start.4 = ((f32[8,40,128]{2,1,0:T(8,128)}), f32[8,40,128]{2,1,0:T(8,128)S(1)}, u32[]{:S(2)}, u32[]{:S(2)}) async-start(f32[8,40,128]{2,1,0:T(8,128)} %broadcast_in_dim.125), calls=%async_computation.4 | async-start | bytes 327680 | tf_op jit(solution)/shard_map/all_to_all | solution.py:225
  210.8 0.7 broadcast_subtract_fusion
  211.5 8.7 %all-to-all-done.4 = f32[8,40,128]{2,1,0:T(8,128)S(1)} async-done(((f32[8,40,128]{2,1,0:T(8,128)}), f32[8,40,128]{2,1,0:T(8,128)S(1)}, u32[]{:S(2)}, u32[]{:S(2)}) %all-to-all-start.4) | async-done | bytes 163872 | tf_op jit(solution)/shard_map/all_to_all | solution.py:225
  220.2 0.7 copy.31
  (67 shorter events, 3.4 us)
Async XLA Ops:
  3.0 2.5 %copy-start.1 = (bf16[1536,512]{1,0:T(8,128)(2,1)}, bf16[1536,512]{1,0:T(8,128)(2,1)S(1)}, u32[]{:S(2)}) copy-start(bf16[1536,512]{1,0:T(8,128)(2,1)S(1)} %add_convert_fusion) | copy-start | bytes 4718596
  3.0 2.6 %copy-start = (s32[1536,512]{1,0:T(8,128)S(1)}, s32[1536,512]{1,0:T(8,128)}, u32[]{:S(2)}) copy-start(s32[1536,512]{1,0:T(8,128)} %param.4) | copy-start | bytes 9437188
  5.6 1.0 copy-start.4
  6.6 2.9 %copy-start.2 = (s32[1536,128]{1,0:T(8,128)S(1)}, s32[1536,128]{1,0:T(8,128)}, u32[]{:S(2)}) copy-start(s32[1536,128]{1,0:T(8,128)} %param.5) | copy-start | bytes 2359300
  19.4 44.6 %all-to-all-start = ((f32[32,8,1152]{2,1,0:T(8,128)}), f32[32,8,1152]{2,1,0:T(8,128)}, u32[]{:S(2)}, u32[]{:S(2)}) async-start(f32[32,8,1152]{2,1,0:T(8,128)} %pad_maximum_fusion), calls=%async_computation | async-start | bytes 2359296 | tf_op jit(solution)/shard_map/all_to_all | solution.py:108
  68.5 0.6 copy-start.8
  71.6 21.8 %all-to-all-start.1 = ((bf16[32,8,1024]{2,1,0:T(8,128)(2,1)}), bf16[32,8,1024]{2,1,0:T(8,128)(2,1)}, u32[]{:S(2)}, u32[]{:S(2)}) async-start(bf16[32,8,1024]{2,1,0:T(8,128)(2,1)} %broadcast_in_dim.108), calls=%async_computation.1 | async-start | bytes 1048576 | tf_op jit(solution)/shard_map/all_to_all | solution.py:156
  107.4 2.6 %copy-start.5 = (bf16[256,512]{1,0:T(8,128)(2,1)S(1)}, bf16[256,512]{1,0:T(8,128)(2,1)}, u32[]{:S(2)}) copy-start(bf16[256,512]{1,0:T(8,128)(2,1)} %concatenate.57) | copy-start | bytes 786436
  107.4 2.6 %copy-start.6 = (bf16[256,256]{0,1:T(8,128)(2,1)S(1)}, bf16[256,256]{0,1:T(8,128)(2,1)}, u32[]{:S(2)}) copy-start(bf16[256,256]{0,1:T(8,128)(2,1)} %copy.34) | copy-start | bytes 393220
  107.4 2.6 %copy-start.7 = (bf16[256,256]{1,0:T(8,128)(2,1)S(1)}, bf16[256,256]{1,0:T(8,128)(2,1)}, u32[]{:S(2)}) copy-start(bf16[256,256]{1,0:T(8,128)(2,1)} %get-tuple-element.17) | copy-start | bytes 393220
  109.8 0.7 copy-start.9
  109.9 0.7 copy-start.10
  109.9 0.7 copy-start.11
  109.9 0.7 copy-start.12
  109.9 0.7 copy-start.13
  109.9 0.7 copy-start.14
  122.5 3.8 %collective-permute-start = (bf16[160,1536]{1,0:T(8,128)(2,1)S(1)}, bf16[160,1536]{1,0:T(8,128)(2,1)S(1)}, u32[]{:S(2)}, u32[]{:S(2)}) collective-permute-start(bf16[160,1536]{1,0:T(8,128)(2,1)S(1)} %convolution_convert_fusion), channel_id=1, source_target_pairs={{0,1},{1,0},{2,3},{3,2},{4,5},{5,4},{6,7},{7,6},{8,9},{9,8},{10,11... | collective-permute-start | bytes 1474568 | tf_op jit(solution)/shard_map/ppermute | solution.py:207
  129.8 25.3 %all-to-all-start.2 = ((bf16[8,20,1536]{2,1,0:T(8,128)(2,1)}), bf16[8,20,1536]{2,1,0:T(8,128)(2,1)S(1)}, u32[]{:S(2)}, u32[]{:S(2)}) async-start(bf16[8,20,1536]{2,1,0:T(8,128)(2,1)} %reshape.255), calls=%async_computation.2 | async-start | bytes 1179648 | tf_op jit(solution)/shard_map/all_to_all | solution.py:209
  155.2 19.7 %copy-start.3 = (s32[1536,128]{1,0:T(8,128)S(1)}, s32[1536,128]{1,0:T(8,128)}, u32[]{:S(2)}) copy-start(s32[1536,128]{1,0:T(8,128)} %param.5) | copy-start | bytes 2359300
  176.0 15.2 %all-to-all-start.3 = ((f32[8,48,128]{2,1,0:T(8,128)}), f32[8,48,128]{2,1,0:T(8,128)S(1)}, u32[]{:S(2)}, u32[]{:S(2)}) async-start(f32[8,48,128]{2,1,0:T(8,128)} %select_maximum_fusion), calls=%async_computation.3 | async-start | bytes 393216 | tf_op jit(solution)/shard_map/all_to_all | solution.py:221
  207.4 12.7 %all-to-all-start.4 = ((f32[8,40,128]{2,1,0:T(8,128)}), f32[8,40,128]{2,1,0:T(8,128)S(1)}, u32[]{:S(2)}, u32[]{:S(2)}) async-start(f32[8,40,128]{2,1,0:T(8,128)} %broadcast_in_dim.125), calls=%async_computation.4 | async-start | bytes 327680 | tf_op jit(solution)/shard_map/all_to_all | solution.py:225
where the time goes:
time: 223 us; the launch traced here: 221 us
  waiting for transfers between devices  83.4 us (37%)
  starting transfers between devices  35.7 us (16%)
  blocking collectives  34.5 us (15%)
  local copies, waits for them, and re-layouts  25.3 us (11%)
  other arithmetic  20.5 us (9%)
  matrix products  20 us (9%)
    all_to_all x1, waiting for transfers between devices, shards(): chunk = jnp.sum(lax.all_to_all(payload, SAMP, 0, 0, tiled=True), axis=0)  30.3 us
    dot_general x9, matrix products, dot(): lax.dot_general(a, b, (contract, ((), ())), precision=precision, preferre...  20 us
    all_gather x1, blocking collectives, shards(): lax.all_gather(residual.astype(BF16).reshape(RIDGE * share, rows), BLK, a...  19.1 us
    all_to_all x1, waiting for transfers between devices, shards(): summed = lax.all_to_all(paired, 'y', 0, 0, tiled=True)  16.9 us
    psum x1, blocking collectives, shards(): ends = lax.psum(ends, 'x')  15.4 us
    all_to_all x1, waiting for transfers between devices, shards(): lax.all_to_all(jnp.broadcast_to(own_rows[None], (samp, *own_rows.shape)),...  14.7 us
    all_to_all x1, starting transfers between devices, shards(): chunk = jnp.sum(lax.all_to_all(payload, SAMP, 0, 0, tiled=True), axis=0)  13.3 us
    all_to_all x1, waiting for transfers between devices, shards(): ends = jnp.sum(lax.all_to_all(ends, 'z', 0, 0, tiled=True), axis=0)  11 us
  transfers between devices with their start and end apart: 6, of which 6 were waited for; matrix products, arithmetic and copies ran while one was open for 2% of the time, Pallas kernels for 0%

commit v1 on v0

--- a/solution.py
+++ b/solution.py
@@ -219,7 +219,7 @@
     squares = jnp.pad(squares, ((0, 0), (0, 7), (0, fresh_width - columns // zs)))
     ends = jnp.concatenate([raw_part.reshape(zs, columns // zs, fresh_width), squares], axis=1)
     ends = jnp.sum(lax.all_to_all(ends, "z", 0, 0, tiled=True), axis=0)
-    ends = lax.psum(ends, "x")
+    ends = jnp.sum(lax.all_gather(ends, "x"), axis=0)
     raw, sum_sq = (ends[: columns // zs], ends[columns // zs, : columns // zs])
     scores = raw / jnp.sqrt(count * (sum_sq / count + EPS))[:, None]
     scores = lax.all_to_all(

time: 223 us -> 219 us (0.982)
  blocking collectives: 34.5 us -> 31 us
    psum x1 -> x0, blocking collectives: 15.4 us -> none  [shards(): ends = lax.psum(ends, 'x')]
    all_gather x0 -> x1, blocking collectives: none -> 11.9 us  [shards(): ends = jnp.sum(lax.all_gather(ends, 'x'), axis=0)]
where the time goes in v1:
time: 219 us; the launch traced here: 217 us
  waiting for transfers between devices  83.4 us (38%)
  starting transfers between devices  35.7 us (16%)
  blocking collectives  31 us (14%)
  local copies, waits for them, and re-layouts  25.3 us (12%)
  other arithmetic  20.5 us (9%)
  matrix products  20 us (9%)
    all_to_all x1, waiting for transfers between devices, shards(): chunk = jnp.sum(lax.all_to_all(payload, SAMP, 0, 0, tiled=True), axis=0)  30.3 us
    dot_general x9, matrix products, dot(): lax.dot_general(a, b, (contract, ((), ())), precision=precision, preferre...  20 us
    all_gather x1, blocking collectives, shards(): lax.all_gather(residual.astype(BF16).reshape(RIDGE * share, rows), BLK, a...  19.1 us
    all_to_all x1, waiting for transfers between devices, shards(): summed = lax.all_to_all(paired, 'y', 0, 0, tiled=True)  16.9 us
    all_to_all x1, waiting for transfers between devices, shards(): lax.all_to_all(jnp.broadcast_to(own_rows[None], (samp, *own_rows.shape)),...  14.7 us
    all_to_all x1, starting transfers between devices, shards(): chunk = jnp.sum(lax.all_to_all(payload, SAMP, 0, 0, tiled=True), axis=0)  13.3 us
    all_gather x1, blocking collectives, shards(): ends = jnp.sum(lax.all_gather(ends, 'x'), axis=0)  11.9 us
    all_to_all x1, waiting for transfers between devices, shards(): ends = jnp.sum(lax.all_to_all(ends, 'z', 0, 0, tiled=True), axis=0)  11 us
  transfers between devices with their start and end apart: 6, of which 6 were waited for; matrix products, arithmetic and copies ran while one was open for 2% of the time, Pallas kernels for 0%

profile of v1, /device:TPU:8, one launch (start us, length us, event | category | flops | bytes accessed | tf_op | source)
XLA Modules:
  0.0 217.4 jit_solution(13916827593753501115)
XLA Ops:
  0.6 2.3 %add_convert_fusion = bf16[1536,512]{1,0:T(8,128)(2,1)S(1)} fusion(s32[1536,512]{1,0:T(8,128)} %param.4), kind=kLoop, calls=%fused_computation.3 | loop fusion | flops 1572864 | bytes 4718592 | tf_op jit(solution)/shard_map/convert_element_type | solution.py:82
  3.0 1.4 fusion.2
  4.4 1.1 fusion
  5.6 0.6 multiply_reduce_fusion
  6.6 2.1 fusion.119
  8.8 0.7 fusion.171
  9.8 1.3 constant_dynamic-update-slice_fusion.4
  11.1 1.3 constant_dynamic-update-slice_fusion.3
  12.4 1.3 constant_dynamic-update-slice_fusion.2
  13.6 1.3 constant_dynamic-update-slice_fusion.1
  14.9 1.3 constant_dynamic-update-slice_fusion
  16.2 0.7 pad.8
  16.9 1.4 maximum_bitcast_fusion
  18.3 1.1 pad_maximum_fusion
  19.4 13.3 %all-to-all-start = ((f32[32,8,1152]{2,1,0:T(8,128)}), f32[32,8,1152]{2,1,0:T(8,128)}, u32[]{:S(2)}, u32[]{:S(2)}) async-start(f32[32,8,1152]{2,1,0:T(8,128)} %pad_maximum_fusion), calls=%async_computation | async-start | bytes 2359296 | tf_op jit(solution)/shard_map/all_to_all | solution.py:108
  32.7 0.5 iota_add_fusion.2
  33.2 0.5 iota_add_fusion.1
  33.7 30.3 %all-to-all-done = f32[32,8,1152]{2,1,0:T(8,128)} async-done(((f32[32,8,1152]{2,1,0:T(8,128)}), f32[32,8,1152]{2,1,0:T(8,128)}, u32[]{:S(2)}, u32[]{:S(2)}) %all-to-all-start) | async-done | bytes 1179680 | tf_op jit(solution)/shard_map/all_to_all | solution.py:108
  64.0 2.0 reduce_sum.106
  66.0 0.8 slice_bitcast_fusion.1
  67.0 0.7 slice_multiply_fusion.4
  67.7 0.8 fusion.131
  68.5 0.6 copy-done.8
  69.1 0.8 fusion.138
  69.9 0.8 fusion.126
  70.8 0.9 broadcast_in_dim.108
  71.6 5.3 %all-to-all-start.1 = ((bf16[32,8,1024]{2,1,0:T(8,128)(2,1)}), bf16[32,8,1024]{2,1,0:T(8,128)(2,1)}, u32[]{:S(2)}, u32[]{:S(2)}) async-start(bf16[32,8,1024]{2,1,0:T(8,128)(2,1)} %broadcast_in_dim.108), calls=%async_computation.1 | async-start | bytes 1048576 | tf_op jit(solution)/shard_map/all_to_all | solution.py:156
  77.0 0.6 fusion.148
  77.6 0.6 iota_divide_fusion
  78.2 0.6 fusion.145
  78.7 14.7 %all-to-all-done.1 = bf16[32,8,1024]{2,1,0:T(8,128)(2,1)} async-done(((bf16[32,8,1024]{2,1,0:T(8,128)(2,1)}), bf16[32,8,1024]{2,1,0:T(8,128)(2,1)}, u32[]{:S(2)}, u32[]{:S(2)}) %all-to-all-start.1) | async-done | bytes 524320 | tf_op jit(solution)/shard_map/all_to_all | solution.py:156
  93.5 1.8 fusion.170
  95.3 1.7 concatenate.57
  96.9 1.7 copy.42
  98.6 1.2 abs_reduce_fusion
  99.8 0.6 reduce_sum.108
  100.4 1.4 fusion.150
  102.4 0.7 negate_multiply_fusion
  103.0 0.7 add_add_fusion.1
  103.7 0.7 fusion.176
  104.4 0.7 fusion.177
  105.1 0.7 fusion.175
  105.7 1.7 copy.36
  107.4 0.9 fusion.172
  108.5 1.3 fusion.111
  110.6 11.3 %convolution_convert_fusion.1 = bf16[320,512]{1,0:T(8,128)(2,1)S(1)} fusion(f32[64,512]{1,0:T(8,128)S(1)} %fusion.109, f32[64,512]{1,0:T(8,128)S(1)} %get-tuple-element.14, f32[64,512]{1,0:T(8,128)S(1)} %get-tuple-element.20, f32[]{:T(128)} %bitcast.18, f32[]{:T(128)} %bitcast.17, f32[]{:T(128)} %bitcast.16, f32[]{:T(128)} %bitcast.15, f32[]{:T(128)} %bitcast.14, ...), kind=kOutput, calls=%fused_computation.6 | convolution fusion | flops 383008768 | bytes 726720 | tf_op jit(solution)/shard_map/dot_general | solution.py:16
  121.8 0.7 convolution_convert_fusion
  122.5 1.9 collective-permute-start
  124.5 1.8 collective-permute-done
  126.3 1.5 add_convert_fusion.1
  127.8 2.0 reshape.255
  129.8 7.5 %all-to-all-start.2 = ((bf16[8,20,1536]{2,1,0:T(8,128)(2,1)}), bf16[8,20,1536]{2,1,0:T(8,128)(2,1)S(1)}, u32[]{:S(2)}, u32[]{:S(2)}) async-start(bf16[8,20,1536]{2,1,0:T(8,128)(2,1)} %reshape.255), calls=%async_computation.2 | async-start | bytes 1179648 | tf_op jit(solution)/shard_map/all_to_all | solution.py:209
  137.4 0.8 add_multiply_fusion.4
  138.1 16.9 %all-to-all-done.2 = bf16[8,20,1536]{2,1,0:T(8,128)(2,1)S(1)} async-done(((bf16[8,20,1536]{2,1,0:T(8,128)(2,1)}), bf16[8,20,1536]{2,1,0:T(8,128)(2,1)S(1)}, u32[]{:S(2)}, u32[]{:S(2)}) %all-to-all-start.2) | async-done | bytes 491552 | tf_op jit(solution)/shard_map/all_to_all | solution.py:209
  155.2 19.1 %all-gather.1 = bf16[16,20,1536]{2,1,0:T(8,128)(2,1)S(1)} all-gather(bf16[1,20,1536]{2,1,0:T(8,128)(2,1)S(1)} %fusion.121), channel_id=1, replica_groups=mesh['x'=4,'z'=8,'y'=8,'core'=2] {'y','core'}, dimensions={0}, use_global_device_ids=true | all-gather | bytes 1044480 | tf_op jit(solution)/shard_map/all_gather | solution.py:213
  175.3 0.7 select_maximum_fusion
  176.0 4.2 %all-to-all-start.3 = ((f32[8,48,128]{2,1,0:T(8,128)}), f32[8,48,128]{2,1,0:T(8,128)S(1)}, u32[]{:S(2)}, u32[]{:S(2)}) async-start(f32[8,48,128]{2,1,0:T(8,128)} %select_maximum_fusion), calls=%async_computation.3 | async-start | bytes 393216 | tf_op jit(solution)/shard_map/all_to_all | solution.py:221
  180.3 11.0 %all-to-all-done.3 = f32[8,48,128]{2,1,0:T(8,128)S(1)} async-done(((f32[8,48,128]{2,1,0:T(8,128)}), f32[8,48,128]{2,1,0:T(8,128)S(1)}, u32[]{:S(2)}, u32[]{:S(2)}) %all-to-all-start.3) | async-done | bytes 196640 | tf_op jit(solution)/shard_map/all_to_all | solution.py:221
  191.3 11.9 %all-gather = f32[192,128]{1,0:T(8,128)S(1)} all-gather(f32[48,128]{1,0:T(8,128)S(1)} %reduce_sum.111), channel_id=2, replica_groups=mesh['x'=4,'z'=8,'y'=8,'core'=2] {'x'}, dimensions={0}, use_global_device_ids=true | all-gather | bytes 122880 | tf_op jit(solution)/shard_map/all_gather | solution.py:222
  203.3 0.7 broadcast_in_dim.125
  204.0 3.4 %all-to-all-start.4 = ((f32[8,40,128]{2,1,0:T(8,128)}), f32[8,40,128]{2,1,0:T(8,128)S(1)}, u32[]{:S(2)}, u32[]{:S(2)}) async-start(f32[8,40,128]{2,1,0:T(8,128)} %broadcast_in_dim.125), calls=%async_computation.4 | async-start | bytes 327680 | tf_op jit(solution)/shard_map/all_to_all | solution.py:225
  207.4 0.7 broadcast_subtract_fusion
  208.0 8.7 %all-to-all-done.4 = f32[8,40,128]{2,1,0:T(8,128)S(1)} async-done(((f32[8,40,128]{2,1,0:T(8,128)}), f32[8,40,128]{2,1,0:T(8,128)S(1)}, u32[]{:S(2)}, u32[]{:S(2)}) %all-to-all-start.4) | async-done | bytes 163872 | tf_op jit(solution)/shard_map/all_to_all | solution.py:225
  216.7 0.7 copy.39
  (68 shorter events, 3.4 us)
Async XLA Ops:
  3.0 2.5 %copy-start.1 = (bf16[1536,512]{1,0:T(8,128)(2,1)}, bf16[1536,512]{1,0:T(8,128)(2,1)S(1)}, u32[]{:S(2)}) copy-start(bf16[1536,512]{1,0:T(8,128)(2,1)S(1)} %add_convert_fusion) | copy-start | bytes 4718596
  3.0 2.6 %copy-start = (s32[1536,512]{1,0:T(8,128)S(1)}, s32[1536,512]{1,0:T(8,128)}, u32[]{:S(2)}) copy-start(s32[1536,512]{1,0:T(8,128)} %param.4) | copy-start | bytes 9437188
  5.6 1.0 copy-start.4
  6.6 2.9 %copy-start.2 = (s32[1536,128]{1,0:T(8,128)S(1)}, s32[1536,128]{1,0:T(8,128)}, u32[]{:S(2)}) copy-start(s32[1536,128]{1,0:T(8,128)} %param.5) | copy-start | bytes 2359300
  19.4 44.6 %all-to-all-start = ((f32[32,8,1152]{2,1,0:T(8,128)}), f32[32,8,1152]{2,1,0:T(8,128)}, u32[]{:S(2)}, u32[]{:S(2)}) async-start(f32[32,8,1152]{2,1,0:T(8,128)} %pad_maximum_fusion), calls=%async_computation | async-start | bytes 2359296 | tf_op jit(solution)/shard_map/all_to_all | solution.py:108
  68.5 0.6 copy-start.8
  71.6 21.8 %all-to-all-start.1 = ((bf16[32,8,1024]{2,1,0:T(8,128)(2,1)}), bf16[32,8,1024]{2,1,0:T(8,128)(2,1)}, u32[]{:S(2)}, u32[]{:S(2)}) async-start(bf16[32,8,1024]{2,1,0:T(8,128)(2,1)} %broadcast_in_dim.108), calls=%async_computation.1 | async-start | bytes 1048576 | tf_op jit(solution)/shard_map/all_to_all | solution.py:156
  107.4 2.6 %copy-start.5 = (bf16[256,512]{1,0:T(8,128)(2,1)S(1)}, bf16[256,512]{1,0:T(8,128)(2,1)}, u32[]{:S(2)}) copy-start(bf16[256,512]{1,0:T(8,128)(2,1)} %concatenate.57) | copy-start | bytes 786436
  107.4 2.6 %copy-start.6 = (bf16[256,256]{0,1:T(8,128)(2,1)S(1)}, bf16[256,256]{0,1:T(8,128)(2,1)}, u32[]{:S(2)}) copy-start(bf16[256,256]{0,1:T(8,128)(2,1)} %copy.42) | copy-start | bytes 393220
  107.4 2.6 %copy-start.7 = (bf16[256,256]{1,0:T(8,128)(2,1)S(1)}, bf16[256,256]{1,0:T(8,128)(2,1)}, u32[]{:S(2)}) copy-start(bf16[256,256]{1,0:T(8,128)(2,1)} %get-tuple-element.17) | copy-start | bytes 393220
  109.8 0.7 copy-start.9
  109.9 0.7 copy-start.10
  109.9 0.7 copy-start.11
  109.9 0.7 copy-start.12
  109.9 0.7 copy-start.13
  109.9 0.7 copy-start.14
  122.5 3.8 %collective-permute-start = (bf16[160,1536]{1,0:T(8,128)(2,1)S(1)}, bf16[160,1536]{1,0:T(8,128)(2,1)S(1)}, u32[]{:S(2)}, u32[]{:S(2)}) collective-permute-start(bf16[160,1536]{1,0:T(8,128)(2,1)S(1)} %convolution_convert_fusion), channel_id=1, source_target_pairs={{0,1},{1,0},{2,3},{3,2},{4,5},{5,4},{6,7},{7,6},{8,9},{9,8},{10,11... | collective-permute-start | bytes 1474568 | tf_op jit(solution)/shard_map/ppermute | solution.py:207
  129.8 25.3 %all-to-all-start.2 = ((bf16[8,20,1536]{2,1,0:T(8,128)(2,1)}), bf16[8,20,1536]{2,1,0:T(8,128)(2,1)S(1)}, u32[]{:S(2)}, u32[]{:S(2)}) async-start(bf16[8,20,1536]{2,1,0:T(8,128)(2,1)} %reshape.255), calls=%async_computation.2 | async-start | bytes 1179648 | tf_op jit(solution)/shard_map/all_to_all | solution.py:209
  155.2 19.7 %copy-start.3 = (s32[1536,128]{1,0:T(8,128)S(1)}, s32[1536,128]{1,0:T(8,128)}, u32[]{:S(2)}) copy-start(s32[1536,128]{1,0:T(8,128)} %param.5) | copy-start | bytes 2359300
  176.0 15.2 %all-to-all-start.3 = ((f32[8,48,128]{2,1,0:T(8,128)}), f32[8,48,128]{2,1,0:T(8,128)S(1)}, u32[]{:S(2)}, u32[]{:S(2)}) async-start(f32[8,48,128]{2,1,0:T(8,128)} %select_maximum_fusion), calls=%async_computation.3 | async-start | bytes 393216 | tf_op jit(solution)/shard_map/all_to_all | solution.py:221
  204.0 12.7 %all-to-all-start.4 = ((f32[8,40,128]{2,1,0:T(8,128)}), f32[8,40,128]{2,1,0:T(8,128)S(1)}, u32[]{:S(2)}, u32[]{:S(2)}) async-start(f32[8,40,128]{2,1,0:T(8,128)} %broadcast_in_dim.125), calls=%async_computation.4 | async-start | bytes 327680 | tf_op jit(solution)/shard_map/all_to_all | solution.py:225
